TPU v7x, 32 devices: a whole 2x2x4 slice. The times are simulated.
32 devices in a mesh: dp: 8 (over y, x, core), mp: 4 (over z).
Axes of the slice: x: 2, y: 2, z: 4, core: 2. Of those that a mesh axis runs over, the one named last changes fastest.
Arguments:
- inputs: bfloat16 [16, 1024, 2048], P('dp', 'mp'), may hold values from -6 to 6
- segment_ids: int32 [16, 1024], P('dp'), may hold values from 0 to 7, never falling along the last dimension, each value on 1 to 512 neighbouring positions
- cotangent: bfloat16 [16, 1024, 2048], P('dp', 'mp'), may hold values from -6 to 6
- query_weight: bfloat16 [2048, 2048], P('dp', 'mp'), may hold values from -0.125 to 0.125
- key_weight: bfloat16 [2048, 2048], P('dp', 'mp'), may hold values from -0.125 to 0.125
- value_weight: bfloat16 [2048, 2048], P('dp', 'mp'), may hold values from -0.125 to 0.125
- out_weight: bfloat16 [2048, 2048], P('mp', 'dp'), may hold values from -0.75 to 0.75
- up_weight: bfloat16 [2048, 8192], P('dp', 'mp'), may hold values from -0.125 to 0.125
- down_weight: bfloat16 [8192, 2048], P('mp', 'dp'), may hold values from -0.0625 to 0.0625
- query_bias: float32 [2048], replicated, may hold values from -3 to 3
- value_bias: float32 [2048], replicated, may hold values from -3 to 3
- out_bias: float32 [2048], replicated, may hold values from -2 to 2
- up_bias: float32 [8192], replicated, may hold values from -3 to 3
- down_bias: float32 [2048], replicated, may hold values from -2 to 2
- first_gain: float32 [2048], replicated, may hold values from 0.1 to 1.9
- first_shift: float32 [2048], replicated, may hold values from -2 to 2
- second_gain: float32 [2048], replicated, may hold values from 0.1 to 1.9
- second_shift: float32 [2048], replicated, may hold values from -2 to 2
Outputs:
- outputs: bfloat16 [16, 1024, 2048], P('dp', 'mp')
- grad_inputs: float32 [16, 1024, 2048], P('dp', 'mp')
- grad_query_weight: float32 [2048, 2048], P('dp', 'mp')
- grad_key_weight: float32 [2048, 2048], P('dp', 'mp')
- grad_value_weight: float32 [2048, 2048], P('dp', 'mp')
- grad_out_weight: float32 [2048, 2048], P('mp', 'dp')
- grad_up_weight: float32 [2048, 8192], P('dp', 'mp')
- grad_down_weight: float32 [8192, 2048], P('mp', 'dp')
- grad_query_bias: float32 [2048], replicated
- grad_value_bias: float32 [2048], replicated
- grad_out_bias: float32 [2048], replicated
- grad_up_bias: float32 [8192], replicated
- grad_down_bias: float32 [2048], replicated
- grad_first_gain: float32 [2048], replicated
- grad_first_shift: float32 [2048], replicated
- grad_second_gain: float32 [2048], replicated
- grad_second_shift: float32 [2048], replicated
Inputs may be any that keep to these rules, and one draw needn't show every extreme that they name: `segment_ids`: along each sequence the numbers never fall; each document holds 1 to 512 tokens, and one of each sequence holds exactly 512.
All inputs are finite; a program needn't handle non-finite values.
Results may differ from a plain program's by a relative error of at most 0.014.
Values may be sent and summed in bfloat16 or wider, within the bound.
A program may use at most 320 MiB of HBM per device.

v0:
```python
import functools

import jax
import jax.numpy as jnp
from jax import lax
from jax.experimental import pallas as pl
from jax.experimental.pallas import tpu as pltpu
from jax.sharding import PartitionSpec as P


HEAD_DIM = 128
SCALING = HEAD_DIM ** (-0.5)
EPSILON = 1e-12
MASKED = -1e30
LOW = jnp.bfloat16
WIDE = jnp.float32


def contract(left, right, left_dim, right_dim):
    return lax.dot_general(
        left, right, (((left_dim,), (right_dim,)), ((), ())), preferred_element_type=WIDE
    )


def norm_forward(resid, scale_vec, shift_vec):
    average = jnp.mean(resid, axis=-1, keepdims=True)
    centered = resid - average
    variance = jnp.mean(centered * centered, axis=-1, keepdims=True)
    inv_std = lax.rsqrt(variance + EPSILON)
    normed = centered * inv_std
    return normed * scale_vec + shift_vec, normed, inv_std


def norm_backward(upstream, normed, inv_std, scale_vec):
    scaled = upstream * scale_vec
    first_mean = jnp.mean(scaled, axis=-1, keepdims=True)
    second_mean = jnp.mean(scaled * normed, axis=-1, keepdims=True)
    return inv_std * (scaled - first_mean - normed * second_mean)


def gelu_tanh(values_in):
    return jax.nn.gelu(values_in, approximate=True)


def head_rows(refs, column):
    return jnp.concatenate([ref[:, column : column + HEAD_DIM] for ref in refs], axis=0)


def forward_kernel(heads, parts, which, *refs):
    qkv_refs = refs[:parts]
    keys_segment, query_segments, out_ref, lse_ref = refs[parts:]
    segment_col = keys_segment[0]
    segment_row = query_segments[0, which : which + 1]
    allowed = segment_col == segment_row
    for head in range(heads):
        queries = qkv_refs[which][:, head * HEAD_DIM : (head + 1) * HEAD_DIM]
        keys_all = head_rows(qkv_refs, (heads + head) * HEAD_DIM)
        values_all = head_rows(qkv_refs, (2 * heads + head) * HEAD_DIM)
        logits = jnp.where(allowed, contract(keys_all, queries, 1, 1) * SCALING, MASKED)
        top = jnp.max(logits, axis=0, keepdims=True)
        expo = jnp.exp(logits - top)
        total = jnp.sum(expo, axis=0, keepdims=True)
        probs_low = (expo * (1.0 / total)).astype(LOW)
        mixed = contract(values_all, probs_low, 0, 0)
        out_ref[:, head * HEAD_DIM : (head + 1) * HEAD_DIM] = mixed.T.astype(LOW)
        lse_ref[0, head : head + 1] = top + jnp.log(total)


def backward_kernel(heads, parts, *refs):
    qkv_refs = refs[:parts]
    grad_refs = refs[parts : 2 * parts]
    lse_refs = refs[2 * parts : 3 * parts]
    keys_segment, query_segments = refs[3 * parts : 3 * parts + 2]
    out_refs = refs[3 * parts + 2 : 4 * parts + 2]
    bias_ref = refs[4 * parts + 2]
    rows = qkv_refs[0].shape[0]
    segment_col = keys_segment[0]
    bias_ref[...] = jnp.zeros_like(bias_ref)
    for head in range(heads):
        base = head * HEAD_DIM
        keys_all = head_rows(qkv_refs, heads * HEAD_DIM + base)
        values_all = head_rows(qkv_refs, 2 * heads * HEAD_DIM + base)
        grad_keys = 0.0
        grad_values = 0.0
        query_bias = 0.0
        for which in range(parts):
            queries = qkv_refs[which][:, base : base + HEAD_DIM]
            grad_mixed = grad_refs[which][:, base : base + HEAD_DIM]
            allowed = segment_col == query_segments[0, which : which + 1]
            logits = contract(keys_all, queries, 1, 1) * SCALING
            probs = jnp.where(allowed, jnp.exp(logits - lse_refs[which][0, head : head + 1]), 0.0)
            grad_probs = contract(values_all, grad_mixed, 1, 1)
            inner = jnp.sum(probs * grad_probs, axis=0, keepdims=True)
            grad_logits = (probs * (grad_probs - inner)).astype(LOW)
            probs_low = probs.astype(LOW)
            grad_values = grad_values + jnp.dot(
                probs_low, grad_mixed, preferred_element_type=WIDE
            )
            grad_keys = grad_keys + jnp.dot(grad_logits, queries, preferred_element_type=WIDE)
            grad_queries = (contract(keys_all, grad_logits, 0, 0) * SCALING).T.astype(LOW)
            query_bias = query_bias + jnp.sum(grad_queries.astype(WIDE), axis=0, keepdims=True)
            out_refs[which][:, base : base + HEAD_DIM] = grad_queries
        grad_keys = (grad_keys * SCALING).astype(LOW)
        grad_values = grad_values.astype(LOW)
        bias_ref[0, :, base : base + HEAD_DIM] = query_bias
        start = 2 * heads * HEAD_DIM + base
        bias_ref[0, :, start : start + HEAD_DIM] = jnp.sum(
            grad_values.astype(WIDE), axis=0, keepdims=True
        )
        for which in range(parts):
            piece = slice(which * rows, (which + 1) * rows)
            start = heads * HEAD_DIM + base
            out_refs[which][:, start : start + HEAD_DIM] = grad_keys[piece]
            start = 2 * heads * HEAD_DIM + base
            out_refs[which][:, start : start + HEAD_DIM] = grad_values[piece]


def row_spec(rows, width):
    return pl.BlockSpec((rows, width), lambda s: (s, 0))


def cube_spec(*dims):
    return pl.BlockSpec((1,) + dims, lambda s: (s, 0, 0))


def attend_forward(which, qkv, segment_cols, segment_rows):
    parts = len(qkv)
    seqs, _, rows = segment_rows.shape
    width = qkv[0].shape[1] // 3
    heads = width // HEAD_DIM
    pairs = seqs * heads * rows * rows * parts
    return pl.pallas_call(
        functools.partial(forward_kernel, heads, parts, which),
        grid=(seqs,),
        in_specs=[row_spec(rows, 3 * width)] * parts
        + [cube_spec(parts * rows, 1), cube_spec(parts, rows)],
        out_specs=[row_spec(rows, width), cube_spec(heads, rows)],
        out_shape=[
            jax.ShapeDtypeStruct((seqs * rows, width), LOW),
            jax.ShapeDtypeStruct((seqs, heads, rows), WIDE),
        ],
        cost_estimate=pl.CostEstimate(
            flops=4 * pairs * HEAD_DIM,
            bytes_accessed=8 * seqs * rows * width * parts,
            transcendentals=pairs,
        ),
        compiler_params=pltpu.CompilerParams(vmem_limit_bytes=56 << 20),
        name="attend_forward",
    )(*qkv, segment_cols, segment_rows)


def attend_backward(qkv, grads, lses, segment_cols, segment_rows):
    parts = len(qkv)
    seqs, _, rows = segment_rows.shape
    width = qkv[0].shape[1] // 3
    heads = width // HEAD_DIM
    pairs = seqs * heads * rows * rows * parts * parts
    results = pl.pallas_call(
        functools.partial(backward_kernel, heads, parts),
        grid=(seqs,),
        in_specs=[row_spec(rows, 3 * width)] * parts
        + [row_spec(rows, width)] * parts
        + [cube_spec(heads, rows)] * parts
        + [cube_spec(parts * rows, 1), cube_spec(parts, rows)],
        out_specs=[row_spec(rows, 3 * width)] * parts + [cube_spec(1, 3 * width)],
        out_shape=[jax.ShapeDtypeStruct((seqs * rows, 3 * width), LOW)] * parts
        + [jax.ShapeDtypeStruct((seqs, 1, 3 * width), WIDE)],
        cost_estimate=pl.CostEstimate(
            flops=10 * pairs * HEAD_DIM,
            bytes_accessed=16 * seqs * rows * width * parts,
            transcendentals=pairs,
        ),
        compiler_params=pltpu.CompilerParams(vmem_limit_bytes=56 << 20),
        name="attend_backward",
    )(*qkv, *grads, *lses, segment_cols, segment_rows)
    return list(results[:parts]), jnp.sum(results[parts], axis=(0, 1))


together = lax.optimization_barrier


def scatter_plan(bits, parts):
    plan = []
    for part in range(parts):
        order = bits if part % 2 == 0 else bits[::-1]
        held = patterns_of(bits)
        for bit in order:
            plan.append((part, bit, tuple(p for p in held if p & bit)))
            held = [p for p in held if not p & bit]
    return plan


def patterns_of(bits):
    patterns = [0]
    for bit in bits:
        patterns += [p | bit for p in patterns]
    return patterns


def scatter_kernel(bits, parts, side, *refs):
    left_refs, right_ref, refs = refs[:parts], refs[parts], refs[parts + 1 :]
    if side:
        stream_refs, out_ref, term_ref, refs = refs[:parts], refs[parts], refs[parts + 1], refs[parts + 2 :]
        streamed, term_sum, term_low, stream_sems, term_sems = refs[8:]
    else:
        out_ref, refs = refs[0], refs[1:]
    far, arrived, held, passed, core_send, core_recv, ring_send, ring_recv = refs[:8]
    rank = lax.axis_index("dp")
    block, width = out_ref.shape[1:]
    stride = min(512, width)

    def across(bit):
        return rank + bit - 2 * bit * (rank // bit % 2)

    barrier = pltpu.get_barrier_semaphore()
    partners = [1] + list(bits)
    for bit in partners:
        pl.semaphore_signal(
            barrier,
            inc=1,
            device_id={"dp": across(bit)},
            device_id_type=pl.DeviceIdType.MESH,
        )
    pl.semaphore_wait(barrier, len(partners))

    patterns = patterns_of(bits)
    place = {p: k for k, p in enumerate(patterns)}

    def tile_rows(part, pattern):
        owner = rank
        for bit in partners:
            if pattern & bit:
                owner = owner + bit - 2 * bit * (rank // bit % 2)
        return left_refs[part].at[pl.ds(pl.multiple_of(owner * block, block), block)]

    def by_columns(function):
        @pl.loop(0, width // stride)
        def _(step):
            function(pl.ds(pl.multiple_of(step * stride, stride), stride))

    deep = left_refs[0].shape[1]
    half_rows = left_refs[0].shape[0] // 2
    lanes = 256 if deep % 256 == 0 else 128
    turns = 2 * (width // stride)

    def stream_copy(part, turn):
        return pltpu.make_async_copy(
            stream_refs[part].at[
                pl.ds(pl.multiple_of(turn % 2 * half_rows, half_rows), half_rows),
                pl.ds(pl.multiple_of(turn // 2 * stride, stride), stride),
            ],
            streamed.at[turn % 2 * parts + part],
            stream_sems.at[turn % 2 * parts + part],
        )

    def term_copy(column):
        return pltpu.make_async_copy(
            term_low.at[column % 2],
            term_ref.at[:, pl.ds(pl.multiple_of(column * stride, stride), stride)],
            term_sems.at[column % 2],
        )

    def side_work(first_turn, last_turn):
        @pl.loop(first_turn, last_turn)
        def _(turn):
            column = turn // 2
            for part in range(parts):
                stream_copy(part, turn).wait()

            @pl.when(turn + 1 < turns)
            def _():
                for part in range(parts):
                    stream_copy(part, turn + 1).start()

            @pl.when(jnp.logical_and(turn % 2 == 1, column >= 2))
            def _():
                term_copy(column - 2).wait()

            @pl.loop(0, deep // lanes)
            def _(step):
                window = pl.ds(pl.multiple_of(step * lanes, lanes), lanes)
                rows = pl.ds(pl.multiple_of(turn % 2 * half_rows, half_rows), half_rows)
                value = sum(
                    contract(left_refs[part][rows, window], streamed[turn % 2 * parts + part], 0, 0)
                    for part in range(parts)
                )

                @pl.when(turn % 2 == 0)
                def _():
                    term_sum[window] = value

                @pl.when(turn % 2 == 1)
                def _():
                    term_low[column % 2, window] = (term_sum[window] + value).astype(LOW)

            @pl.when(turn % 2 == 1)
            def _():
                term_copy(column).start()

    if side:
        for part in range(parts):
            stream_copy(part, 0).start()

    core_copies = {}
    ring_copies = {}
    slot = 0
    plan = scatter_plan(bits, parts)
    for part, bit, moved in plan:
        for pattern in moved:
            ring_copies[part, bit, pattern] = (
                slot,
                pltpu.make_async_remote_copy(
                    src_ref=held.at[part, place[pattern]],
                    dst_ref=passed.at[slot],
                    send_sem=ring_send.at[slot],
                    recv_sem=ring_recv.at[slot],
                    device_id={"dp": across(bit)},
                    device_id_type=pl.DeviceIdType.MESH,
                ),
            )
            slot += 1

    def far_tile(part, pattern):
        rows = tile_rows(part, pattern | 1)
        index = part * len(patterns) + place[pattern]

        def columns(window):
            far[index, :, window] = jnp.dot(
                rows[...], right_ref[:, window], preferred_element_type=WIDE
            ).astype(LOW)

        by_columns(columns)
        copy = pltpu.make_async_remote_copy(
            src_ref=far.at[index],
            dst_ref=arrived.at[index],
            send_sem=core_send.at[index],
            recv_sem=core_recv.at[index],
            device_id={"dp": across(1)},
            device_id_type=pl.DeviceIdType.MESH,
        )
        copy.start()
        core_copies[part, pattern] = (index, copy)

    def near_tile(part, pattern):
        rows = tile_rows(part, pattern)
        index, copy = core_copies[part, pattern]
        copy.wait_recv()

        def columns(window):
            value = jnp.dot(
                rows[...], right_ref[:, window], preferred_element_type=WIDE
            ) + arrived[index, :, window].astype(WIDE)
            if pattern:
                held[part, place[pattern], :, window] = value.astype(LOW)
            else:
                out_ref[part, :, window] = value

        by_columns(columns)

    def send(part, bit, moved):
        for pattern in moved:
            ring_copies[part, bit, pattern][1].start()

    def take(part, bit, moved):
        for pattern in moved:
            number, copy = ring_copies[part, bit, pattern]
            copy.wait_recv()
            target = pattern - bit

            def columns(window):
                coming = passed[number, :, window].astype(WIDE)
                if target:
                    old = held[part, place[target], :, window].astype(WIDE)
                    held[part, place[target], :, window] = (old + coming).astype(LOW)
                else:
                    out_ref[part, :, window] = out_ref[part, :, window] + coming

            by_columns(columns)

    steps = [[entry for entry in plan if entry[0] == part] for part in range(parts)]
    first = [steps[part][0] for part in range(parts)]
    urgent = [
        (part, pattern)
        for tiles in zip(*[sorted(entry[2], reverse=True) for entry in first])
        for part, pattern in enumerate(tiles)
    ]
    others = [
        (part, pattern)
        for pattern in sorted(patterns, reverse=True)
        for part in range(parts)
        if (part, pattern) not in urgent
    ]
    queue = urgent + others
    ahead = 2 * parts
    for entry in queue[:ahead]:
        far_tile(*entry)
    for number, (part, pattern) in enumerate(queue):
        near_tile(part, pattern)
        if (part, pattern) in urgent:
            ring_copies[part, first[part][1], pattern][1].start()
        if number + ahead < len(queue):
            far_tile(*queue[number + ahead])
    for level in range(len(bits)):
        if side and level < 2:
            cut = [0, turns // 2, turns]
            side_work(cut[level], cut[level + 1])
        for part in range(parts):
            take(*steps[part][level])
            if level + 1 < len(bits):
                send(*steps[part][level + 1])
    if side:
        for column in range(max(0, width // stride - 2), width // stride):
            term_copy(column).wait()
    for _, copy in list(core_copies.values()) + list(ring_copies.values()):
        copy.wait_send()


def product_scatter(lefts, right, collective_id, streams=()):
    parts = len(lefts)
    plane = lax.axis_size("dp")
    bits = [1 << k for k in range(1, plane.bit_length() - 1)]
    rows, depth = lefts[0].shape
    width = right.shape[1]
    block = rows // plane
    tiles = plane // 2
    passes = sum(len(moved) for _, _, moved in scatter_plan(bits, parts))
    sent = parts * tiles * block * width * 2 * 2
    stride = min(512, width)
    side = len(streams) > 0
    vmem, anywhere = (
        pl.BlockSpec(memory_space=pltpu.VMEM),
        pl.BlockSpec(memory_space=pl.ANY),
    )
    side_scratch = [
        pltpu.VMEM((2 * parts, rows // 2, stride), LOW),
        pltpu.VMEM((depth, stride), WIDE),
        pltpu.VMEM((2, depth, stride), LOW),
        pltpu.SemaphoreType.DMA((2 * parts,)),
        pltpu.SemaphoreType.DMA((2,)),
    ]
    result = pl.pallas_call(
        functools.partial(scatter_kernel, bits, parts, side),
        out_shape=[jax.ShapeDtypeStruct((parts, block, width), WIDE)]
        + [jax.ShapeDtypeStruct((depth, width), LOW)] * side,
        in_specs=[vmem] * (parts + 1) + [anywhere] * len(streams),
        out_specs=[vmem] + [anywhere] * side,
        scratch_shapes=[
            pltpu.VMEM((parts * tiles, block, width), LOW),
            pltpu.VMEM((parts * tiles, block, width), LOW),
            pltpu.VMEM((parts, tiles, block, width), LOW),
            pltpu.VMEM((passes, block, width), LOW),
            pltpu.SemaphoreType.DMA((parts * tiles,)),
            pltpu.SemaphoreType.DMA((parts * tiles,)),
            pltpu.SemaphoreType.DMA((passes,)),
            pltpu.SemaphoreType.DMA((passes,)),
        ]
        + side_scratch * side,
        cost_estimate=pl.CostEstimate(
            flops=2 * parts * rows * depth * width * (1 + side),
            bytes_accessed=8 * sent,
            transcendentals=0,
        ),
        compiler_params=pltpu.CompilerParams(
            collective_id=collective_id, has_side_effects=True, vmem_limit_bytes=60 << 20
        ),
        name="product_scatter",
    )(*lefts, right, *streams)
    own = [result[0][b] for b in range(parts)]
    return (own, result[1]) if side else own


ROOT = (2.0 / 3.141592653589793) ** 0.5


def gelu_slope(values_in):
    squared = values_in * values_in
    bend = jnp.tanh(ROOT * values_in * (1.0 + 0.044715 * squared))
    slope = ROOT * (1.0 + 3.0 * 0.044715 * squared)
    return 0.5 * (1.0 + bend) + 0.5 * values_in * (1.0 - bend * bend) * slope


def gather_kernel(bits, parts, mode, *refs):
    backward, plain = mode == "slope", mode == "plain"
    block_refs = refs[:parts]
    weight_ref = refs[parts]
    rest = refs[parts + 1 :]
    if backward:
        wide_refs, rest = rest[:parts], rest[parts:]
        gathered_refs, low_refs, rest = rest[:parts], rest[parts : 2 * parts], rest[2 * parts :]
    elif plain:
        wide_refs = None
        gathered_refs, low_refs, rest = rest[:parts], rest[parts : 2 * parts], rest[2 * parts :]
    else:
        bias_ref, rest = rest[0], rest[1:]
        gathered_refs, wide_refs = rest[:parts], rest[parts : 2 * parts]
        low_refs, rest = rest[2 * parts : 3 * parts], rest[3 * parts :]
    landed, wide_stage, low_stage = rest[:3]
    send_sems, recv_sems, keep_sems, wide_sems, low_sems = rest[3:]
    rank = lax.axis_index("dp")
    block = block_refs[0].shape[0]
    hidden = weight_ref.shape[0]
    stride = min(512, hidden)

    def across(bit):
        return rank + bit - 2 * bit * (rank // bit % 2)

    barrier = pltpu.get_barrier_semaphore()
    partners = [1] + list(bits)
    for bit in partners:
        pl.semaphore_signal(
            barrier,
            inc=1,
            device_id={"dp": across(bit)},
            device_id_type=pl.DeviceIdType.MESH,
        )
    pl.semaphore_wait(barrier, len(partners))

    plane = 1 << len(partners)
    orders = [list(bits) if part % 2 == 0 else list(bits)[::-1] for part in range(parts)]
    near = [patterns_of(order) for order in orders]
    copies = {}

    def slot(part, pattern):
        return part * plane + pattern

    def source(part, pattern):
        return landed.at[slot(part, pattern)] if pattern else block_refs[part]

    def pass_on(part, pattern, bit):
        target = slot(part, pattern | bit)
        copy = pltpu.make_async_remote_copy(
            src_ref=source(part, pattern),
            dst_ref=landed.at[target],
            send_sem=send_sems.at[target],
            recv_sem=recv_sems.at[target],
            device_id={"dp": across(bit)},
            device_id_type=pl.DeviceIdType.MESH,
        )
        copy.start()
        copies[part, pattern | bit] = copy

    def place_of(pattern):
        owner = rank
        for bit in partners:
            if pattern & bit:
                owner = owner + bit - 2 * bit * (rank // bit % 2)
        return pl.ds(pl.multiple_of(owner * block, block), block)

    kept = []

    def keep(part, pattern):
        copy = pltpu.make_async_copy(
            source(part, pattern),
            gathered_refs[part].at[place_of(pattern)],
            keep_sems.at[slot(part, pattern)],
        )
        copy.start()
        kept.append(copy)

    sequence = []
    for turn in range(len(near[0])):
        sequence += [(part, near[part][turn]) for part in range(parts)]
        sequence += [(part, near[part][turn] | 1) for part in range(parts)]
    stored = {}

    def fetch(number):
        part, pattern = sequence[number]
        copy = pltpu.make_async_copy(
            wide_refs[part].at[place_of(pattern)],
            wide_stage.at[number % 2],
            wide_sems.at[number % 2],
        )
        copy.start()
        return copy

    def multiply(number):
        part, pattern = sequence[number]
        turn = number % 2
        rows = source(part, pattern)
        for copy in stored.pop(number - 2, ()):
            copy.wait()
        if backward:
            stored_wide.pop(number).wait()

        @pl.loop(0, hidden // stride)
        def _(step):
            window = pl.ds(pl.multiple_of(step * stride, stride), stride)
            product = contract(rows[...], weight_ref[window], 1, 1)
            if backward:
                value = product * gelu_slope(wide_stage[turn, :, window])
            elif plain:
                value = product
            else:
                value = product + bias_ref[:, window]
                wide_stage[turn, :, window] = value
                value = gelu_tanh(value)
            low_stage[turn, :, window] = value.astype(LOW)

        if backward and number + 2 < len(sequence):
            stored_wide[number + 2] = fetch(number + 2)
        outgoing = [
            pltpu.make_async_copy(
                low_stage.at[turn], low_refs[part].at[place_of(pattern)], low_sems.at[turn]
            )
        ]
        if not backward and not plain:
            outgoing.append(
                pltpu.make_async_copy(
                    wide_stage.at[turn], wide_refs[part].at[place_of(pattern)], wide_sems.at[turn]
                )
            )
        for copy in outgoing:
            copy.start()
        stored[number] = outgoing

    stored_wide = {}
    if backward:
        for number in range(2):
            stored_wide[number] = fetch(number)
    for turn in range(len(bits)):
        for part in range(parts):
            pass_on(part, 0, orders[part][turn])
    for part in range(parts):
        pass_on(part, 0, 1)
        keep(part, 0)

    number = 0
    for turn in range(len(near[0])):
        if turn:
            for part in range(parts):
                pattern = near[part][turn]
                copies[part, pattern].wait_recv()
                highest = max(orders[part].index(bit) for bit in bits if pattern & bit)
                for bit in orders[part][highest + 1 :]:
                    pass_on(part, pattern, bit)
                pass_on(part, pattern, 1)
                keep(part, pattern)
        for part in range(parts):
            multiply(number)
            number += 1
        for part in range(parts):
            pattern = near[part][turn] | 1
            copies[part, pattern].wait_recv()
            keep(part, pattern)
            multiply(number)
            number += 1
    for outgoing in stored.values():
        for copy in outgoing:
            copy.wait()
    for copy in kept:
        copy.wait()
    for copy in copies.values():
        copy.wait_send()


def gather_product(blocks, weight, extra, collective_id):
    mode = "plain" if extra is None else "slope" if isinstance(extra, list) else "bias"
    parts = len(blocks)
    plane = lax.axis_size("dp")
    bits = [1 << k for k in range(1, plane.bit_length() - 1)]
    block, width = blocks[0].shape
    hidden = weight.shape[0]
    rows = plane * block
    vmem, anywhere = (
        pl.BlockSpec(memory_space=pltpu.VMEM),
        pl.BlockSpec(memory_space=pl.ANY),
    )
    gathered = jax.ShapeDtypeStruct((rows, width), LOW)
    wide = jax.ShapeDtypeStruct((rows, hidden), WIDE)
    low = jax.ShapeDtypeStruct((rows, hidden), LOW)
    outs = [gathered] * parts + ([wide] * parts if mode == "bias" else []) + [low] * parts
    extras = {"plain": [], "bias": [extra], "slope": extra}[mode]
    results = pl.pallas_call(
        functools.partial(gather_kernel, bits, parts, mode),
        out_shape=outs,
        in_specs=[vmem] * (parts + 1) + [anywhere if mode == "slope" else vmem] * len(extras),
        out_specs=[anywhere] * len(outs),
        scratch_shapes=[
            pltpu.VMEM((parts * plane, block, width), LOW),
            pltpu.VMEM((2, block, hidden), WIDE),
            pltpu.VMEM((2, block, hidden), LOW),
            pltpu.SemaphoreType.DMA((parts * plane,)),
            pltpu.SemaphoreType.DMA((parts * plane,)),
            pltpu.SemaphoreType.DMA((parts * plane,)),
            pltpu.SemaphoreType.DMA((2,)),
            pltpu.SemaphoreType.DMA((2,)),
        ],
        cost_estimate=pl.CostEstimate(
            flops=2 * parts * rows * hidden * width,
            bytes_accessed=16 * parts * rows * width,
            transcendentals=parts * rows * hidden,
        ),
        compiler_params=pltpu.CompilerParams(
            collective_id=collective_id, has_side_effects=True, vmem_limit_bytes=60 << 20
        ),
        name="gather_product",
    )(*blocks, weight, *extras)
    return [list(results[k : k + parts]) for k in range(0, len(outs), parts)]


def opening_kernel(bits, parts, depth, *refs):
    block_refs, piece_ref = refs[:parts], refs[parts]
    gathered_refs, line_ref = refs[parts + 1 : 2 * parts + 1], refs[2 * parts + 1]
    landed, held_line = refs[2 * parts + 2 : 2 * parts + 4]
    send_sems, recv_sems, keep_sems, line_send, line_recv, line_keep = refs[2 * parts + 4 :]
    rank, level = lax.axis_index("dp"), lax.axis_index("mp")
    block = block_refs[0].shape[0]

    def across(bit):
        return rank + bit - 2 * bit * (rank // bit % 2)

    partners = [1] + list(bits)
    plane = 1 << len(partners)
    barrier = pltpu.get_barrier_semaphore()
    for bit in partners:
        pl.semaphore_signal(
            barrier,
            inc=1,
            device_id={"dp": across(bit)},
            device_id_type=pl.DeviceIdType.MESH,
        )
    for shift in (1, depth - 1):
        pl.semaphore_signal(
            barrier,
            inc=1,
            device_id={"mp": (level + shift) % depth},
            device_id_type=pl.DeviceIdType.MESH,
        )
    pl.semaphore_wait(barrier, len(partners) + 2)

    def line_copy(up, step):
        shard = level - step if up else level + step
        number = step * 2 + (0 if up else 1)
        return pltpu.make_async_remote_copy(
            src_ref=held_line.at[shard] if step else piece_ref,
            dst_ref=held_line.at[shard],
            send_sem=line_send.at[number],
            recv_sem=line_recv.at[number],
            device_id={"mp": (level + (1 if up else depth - 1)) % depth},
            device_id_type=pl.DeviceIdType.MESH,
        )

    def sends(up, step):
        if up:
            return jnp.logical_and(level + 1 < depth, level >= step)
        return jnp.logical_and(level > 0, level + step < depth)

    def receives(up, step):
        return level > step if up else level + step + 1 < depth

    orders = [list(bits) if part % 2 == 0 else list(bits)[::-1] for part in range(parts)]
    near = [patterns_of(order) for order in orders]
    copies = {}

    def place_of(pattern):
        owner = rank
        for bit in partners:
            if pattern & bit:
                owner = owner + bit - 2 * bit * (rank // bit % 2)
        return pl.ds(pl.multiple_of(owner * block, block), block)

    def pass_on(part, pattern, bit):
        target = part * plane + (pattern | bit)
        copy = pltpu.make_async_remote_copy(
            src_ref=landed.at[part * plane + pattern] if pattern else block_refs[part],
            dst_ref=landed.at[target],
            send_sem=send_sems.at[target],
            recv_sem=recv_sems.at[target],
            device_id={"dp": across(bit)},
            device_id_type=pl.DeviceIdType.MESH,
        )
        copy.start()
        copies[part, pattern | bit] = copy

    def line_start(step):
        for up in (True, False):

            @pl.when(sends(up, step))
            def _():
                line_copy(up, step).start()

    line_start(0)
    for turn in range(len(bits)):
        for part in range(parts):
            pass_on(part, 0, orders[part][turn])
    kept = []

    def keep(part, pattern):
        number = part * plane + pattern
        copy = pltpu.make_async_copy(
            landed.at[number] if pattern else block_refs[part],
            gathered_refs[part].at[place_of(pattern)],
            keep_sems.at[number],
        )
        copy.start()
        kept.append(copy)

    def line_keep_copy(up, step):
        shard = level - step if up else level + step
        return pltpu.make_async_copy(
            held_line.at[shard] if step else piece_ref,
            line_ref.at[shard],
            line_keep.at[step * 2 - (0 if up else 1)],
        )

    for part in range(parts):
        pass_on(part, 0, 1)
        keep(part, 0)
    line_keep_copy(True, 0).start()
    for turn in range(1, max(len(near[0]), depth)):
        if turn < len(near[0]):
            for part in range(parts):
                pattern = near[part][turn]
                copies[part, pattern].wait_recv()
                highest = max(orders[part].index(bit) for bit in bits if pattern & bit)
                for bit in orders[part][highest + 1 :]:
                    pass_on(part, pattern, bit)
                pass_on(part, pattern, 1)
                keep(part, pattern)
        if turn < depth:
            for up in (True, False):

                @pl.when(receives(up, turn - 1))
                def _():
                    line_copy(up, turn - 1).wait_recv()
                    line_keep_copy(up, turn).start()

            if turn < depth - 1:
                line_start(turn)
    for part in range(parts):
        for pattern in near[part]:
            copies[part, pattern | 1].wait_recv()
            keep(part, pattern | 1)
    for copy in kept:
        copy.wait()
    for copy in copies.values():
        copy.wait_send()
    line_keep_copy(True, 0).wait()
    for step in range(depth - 1):
        for up in (True, False):

            @pl.when(receives(up, step))
            def _():
                line_keep_copy(up, step + 1).wait()

            @pl.when(sends(up, step))
            def _():
                line_copy(up, step).wait_send()


def opening_gather(blocks, piece, collective_id):
    parts = len(blocks)
    plane, depth = lax.axis_size("dp"), lax.axis_size("mp")
    bits = [1 << k for k in range(1, plane.bit_length() - 1)]
    block, width = blocks[0].shape
    anywhere = pl.BlockSpec(memory_space=pl.ANY)
    results = pl.pallas_call(
        functools.partial(opening_kernel, bits, parts, depth),
        out_shape=[jax.ShapeDtypeStruct((plane * block, width), LOW)] * parts
        + [jax.ShapeDtypeStruct((depth,) + piece.shape, LOW)],
        in_specs=[pl.BlockSpec(memory_space=pltpu.VMEM)] * (parts + 1),
        out_specs=[anywhere] * (parts + 1),
        scratch_shapes=[
            pltpu.VMEM((parts * plane, block, width), LOW),
            pltpu.VMEM((depth,) + piece.shape, LOW),
            pltpu.SemaphoreType.DMA((parts * plane,)),
            pltpu.SemaphoreType.DMA((parts * plane,)),
            pltpu.SemaphoreType.DMA((parts * plane,)),
            pltpu.SemaphoreType.DMA((2 * (depth - 1),)),
            pltpu.SemaphoreType.DMA((2 * (depth - 1),)),
            pltpu.SemaphoreType.DMA((2 * depth - 1,)),
        ],
        cost_estimate=pl.CostEstimate(
            flops=0, bytes_accessed=16 * parts * plane * block * width, transcendentals=0
        ),
        compiler_params=pltpu.CompilerParams(
            collective_id=collective_id, has_side_effects=True, vmem_limit_bytes=60 << 20
        ),
        name="opening_gather",
    )(*blocks, piece)
    return list(results[:parts]), results[parts]


def sum_over(axes, vector):
    for axis in axes:
        size = lax.axis_size(axis)
        step = 1
        while step < size:
            vector = vector + lax.ppermute(vector, axis, [(k, k ^ step) for k in range(size)])
            step *= 2
    return vector


def body(
    inputs,
    segment_ids,
    cotangent,
    query_weight,
    key_weight,
    value_weight,
    out_weight,
    up_weight,
    down_weight,
    query_bias,
    value_bias,
    out_bias,
    up_bias,
    down_bias,
    first_gain,
    first_shift,
    second_gain,
    second_shift,
):
    plane, depth = lax.axis_size("dp"), lax.axis_size("mp")
    rank, level = lax.axis_index("dp"), lax.axis_index("mp")
    parts, block, width = inputs.shape
    length = block * depth
    group = depth // parts
    seqs = plane // group
    rows = group * block
    hidden = up_bias.shape[0] // plane
    heads_in_block = query_weight.shape[1] // HEAD_DIM
    sharers = plane // heads_in_block
    heads = depth // sharers
    parity = level % parts

    def route(turn, back):
        pairs = []
        for i in range(plane):
            for j in range(depth):
                e = (j + turn) % parts
                source = i * depth + j
                target = (i - i % group + j // parts) * depth + parts * (i % group) + e
                pairs.append((target, source) if back else (source, target))
        return pairs

    def pick(options, index):
        return lax.dynamic_index_in_dim(jnp.stack(options), index % parts, 0, keepdims=False)

    def enter(array):
        arrived = [
            lax.ppermute(
                lax.dynamic_index_in_dim(array, (level + turn) % parts, 0, keepdims=False),
                ("dp", "mp"),
                route(turn, False),
            )
            for turn in range(parts)
        ]
        return [pick(arrived, parity - b + parts) for b in range(parts)]

    def leave_picks(blocks):
        return [pick(blocks, parity - turn + parts) for turn in range(parts)]

    def leave_sent(picks):
        return [
            lax.ppermute(picks[turn], ("dp", "mp"), route(turn, True)) for turn in range(parts)
        ]

    def leave_placed(arrived):
        return jnp.stack([pick(arrived, e - parity + parts) for e in range(parts)])

    def swap(array, bit):
        return lax.ppermute(array, "dp", [(k, k ^ bit) for k in range(plane)])

    bits = [1 << k for k in range(plane.bit_length() - 1)]

    sharing = [list(range(k, k + sharers)) for k in range(0, plane, sharers)]

    def share_out(array):
        if sharers == 1:
            return array
        return lax.all_to_all(
            array, "dp", split_axis=0, concat_axis=2, axis_index_groups=sharing, tiled=True
        )

    def share_back(array):
        if sharers == 1:
            return array
        return lax.all_to_all(
            array, "dp", split_axis=2, concat_axis=0, axis_index_groups=sharing, tiled=True
        )

    tokens = enter(inputs)
    attention_shards = jnp.stack([query_weight.T, key_weight.T, value_weight.T, out_weight])
    attention_shards = attention_shards.reshape(4, plane, -1, width // plane)
    attention_pieces = lax.all_to_all(
        attention_shards.transpose(1, 0, 2, 3).reshape(-1, width // plane),
        "dp",
        split_axis=0,
        concat_axis=1,
        tiled=True,
    )
    segments = segment_ids
    for bit in bits:
        other = swap(segments, bit)
        upper = rank // bit % 2 == 1
        segments = jnp.concatenate(
            [jnp.where(upper, other, segments), jnp.where(upper, segments, other)]
        )
    segments = lax.dynamic_index_in_dim(
        segments.reshape(seqs, depth, length), level, 1, keepdims=False
    )
    segments = segments.reshape(seqs, group, parts, block).transpose(0, 2, 1, 3)
    segment_rows = segments.reshape(seqs, parts, rows)
    segment_cols = segments.reshape(seqs, parts * rows, 1)
    tokens, segment_rows, segment_cols = together((tokens, segment_rows, segment_cols))
    forward_shards, attention_pieces = together(((up_weight.T, down_weight), attention_pieces))
    forward_pieces = lax.all_to_all(
        jnp.concatenate(
            [shard.reshape(plane, -1, width // plane) for shard in forward_shards], axis=1
        ).reshape(-1, width // plane),
        "dp",
        split_axis=0,
        concat_axis=1,
        tiled=True,
    )
    gathered_inputs, attention_line = opening_gather(tokens, attention_pieces, 7)
    attention_line, forward_pieces = together((attention_line, forward_pieces))
    up_piece, down_piece = jnp.split(forward_pieces, 2, axis=0)
    attention_full = share_out(attention_line.reshape(depth, 4, -1, width))
    attention_full = attention_full.transpose(1, 0, 2, 3).reshape(4, heads * HEAD_DIM, width)
    full_qkv = attention_full[:3].reshape(3 * heads * HEAD_DIM, width)
    full_out = attention_full[3]

    def own_heads(bias):
        table = bias.reshape(depth, heads_in_block, HEAD_DIM)
        return lax.dynamic_slice(
            table, (rank % sharers * heads, rank // sharers, 0), (heads, 1, HEAD_DIM)
        ).reshape(-1)

    qkv_bias = jnp.concatenate(
        [own_heads(query_bias), jnp.zeros((heads * HEAD_DIM,), WIDE), own_heads(value_bias)]
    )
    own_up = lax.dynamic_slice(
        up_bias.reshape(depth, plane, -1), (0, rank, 0), (depth, 1, hidden // depth)
    ).reshape(-1)

    every = range(parts)
    qkv = [
        (contract(gathered_inputs[b], full_qkv, 1, 1) + qkv_bias).astype(LOW) for b in every
    ]
    full_up = lax.all_gather(up_piece, "mp", axis=0, tiled=True)
    full_down = lax.all_gather(down_piece, "mp", axis=0, tiled=True)
    attended, lses = [], []
    for b in every:
        mixed, lse = attend_forward(b, qkv, segment_cols, segment_rows)
        attended.append(mixed)
        lses.append(lse)
    attn_sums = product_scatter(attended, full_out, 1)
    first = [
        norm_forward(tokens[b].astype(WIDE) + attn_sums[b] + out_bias, first_gain, first_shift)
        for b in every
    ]
    first_low = [first[b][0].astype(LOW) for b in every]
    first_low, full_up, full_down, cotangent = together(
        (first_low, full_up, full_down, cotangent)
    )
    tangents = enter(cotangent)
    gathered_first, up_proj, hiddens = gather_product(
        first_low, full_up, own_up.reshape(1, -1), 4
    )
    hiddens, tangents = together((hiddens, tangents))
    tangents = [array.astype(WIDE) for array in tangents]
    ffn_sums = product_scatter(hiddens, full_down, 2)
    second = [
        norm_forward(first[b][0] + ffn_sums[b] + down_bias, second_gain, second_shift)
        for b in every
    ]
    outputs = leave_placed(
        leave_sent(leave_picks([second[b][0].astype(LOW) for b in every]))
    )

    def share_attention(term):
        return share_back(term.reshape(-1, heads, HEAD_DIM, width).transpose(1, 0, 2, 3))

    def reduce_attention(term):
        return lax.psum_scatter(share_attention(term), "mp", scatter_dimension=0, tiled=True)[0]

    def reduce_forward(term):
        return lax.psum_scatter(term, "mp", scatter_dimension=0, tiled=True)

    def owner_exchange(term):
        return lax.all_to_all(
            term.reshape(-1, width), "dp", split_axis=1, concat_axis=0, tiled=True
        )

    def low_sum(terms):
        return sum(terms).astype(LOW)

    def total(arrays):
        return sum(jnp.sum(array.astype(WIDE), axis=0) for array in arrays)

    grad_second_gain = total([tangents[b] * second[b][1] for b in every])
    grad_second_shift = total(tangents)
    grad_two = [
        norm_backward(tangents[b], second[b][1], second[b][2], second_gain) for b in every
    ]
    grad_ffn = [array.astype(LOW) for array in grad_two]
    grad_down_bias = total(grad_ffn)
    gathered_ffn, grad_upper = gather_product(grad_ffn, full_down, up_proj, 5)
    gathered_ffn, grad_upper, outputs = together((gathered_ffn, grad_upper, outputs))
    grad_up_bias = total(grad_upper)
    back_sums, term_up = product_scatter(grad_upper, full_up, 8, gathered_first)
    term_down = low_sum(contract(hiddens[b], gathered_ffn[b], 0, 0) for b in every)
    grad_first = [grad_two[b] + back_sums[b] for b in every]
    grad_first_gain = total([grad_first[b] * first[b][1] for b in every])
    grad_first_shift = total(grad_first)
    grad_resid = [
        norm_backward(grad_first[b], first[b][1], first[b][2], first_gain) for b in every
    ]
    grad_branch = [array.astype(LOW) for array in grad_resid]
    reduced_down = reduce_forward(term_down)
    grad_branch, reduced_down = together((grad_branch, reduced_down))
    grad_out_bias = total(grad_branch)
    gathered_branch, grad_mixed = gather_product(grad_branch, full_out, None, 6)
    spread_up = lax.dynamic_update_slice(
        jnp.zeros((depth, plane, hidden // depth), WIDE),
        grad_up_bias.reshape(depth, 1, -1),
        (0, rank, 0),
    ).reshape(-1)
    owned_down = owner_exchange(reduced_down)
    reduced_up = reduce_forward(term_up)
    grad_mixed = [
        array.reshape(seqs * rows, heads * HEAD_DIM)
        for array in grad_mixed
    ]
    grad_qkv, grad_qkv_bias = attend_backward(qkv, grad_mixed, lses, segment_cols, segment_rows)

    def spread_heads(piece):
        table = jnp.zeros((depth, heads_in_block, HEAD_DIM), WIDE)
        return lax.dynamic_update_slice(
            table,
            piece.reshape(heads, 1, HEAD_DIM),
            (rank % sharers * heads, rank // sharers, 0),
        ).reshape(-1)

    spread = heads * HEAD_DIM
    vectors = jnp.concatenate(
        [
            spread_heads(grad_qkv_bias[:spread]),
            spread_heads(grad_qkv_bias[2 * spread :]),
            grad_out_bias,
            grad_down_bias,
            grad_first_gain,
            grad_first_shift,
            grad_second_gain,
            grad_second_shift,
            spread_up,
        ]
    )
    vectors = sum_over(("mp",), vectors.reshape(-1, HEAD_DIM))
    reduced_out = reduce_attention(
        low_sum(contract(attended[b], gathered_branch[b], 0, 0) for b in every)
    )
    term_qkv = low_sum(contract(grad_qkv[b], gathered_inputs[b], 0, 0) for b in every)
    term_qkv, reduced_up = together((term_qkv, reduced_up))
    shared_qkv = share_attention(term_qkv)
    owned_up = owner_exchange(reduced_up)
    grad_qkv, shared_qkv, vectors = together((grad_qkv, shared_qkv, vectors))
    input_sums = product_scatter(grad_qkv, full_qkv, 3)
    reduced_qkv = lax.psum_scatter(shared_qkv, "mp", scatter_dimension=0, tiled=True)[0]
    grad_low = [(grad_resid[b] + input_sums[b]).astype(LOW) for b in every]
    leaving = leave_sent(leave_picks(grad_low))
    vectors = sum_over(("dp",), vectors).reshape(-1)
    grad_inputs = leave_placed(leaving).astype(WIDE)

    owned_out = owner_exchange(reduced_out)
    owned_qkv = owner_exchange(reduced_qkv)
    owned_qkv = owned_qkv.reshape(plane, 3, -1, width // plane).transpose(1, 0, 2, 3)
    owned_qkv = owned_qkv.reshape(3, -1, width // plane)

    narrow = vectors[: 8 * width].reshape(8, width)
    return (
        outputs,
        grad_inputs,
        owned_qkv[0].T.astype(WIDE),
        owned_qkv[1].T.astype(WIDE),
        owned_qkv[2].T.astype(WIDE),
        owned_out.astype(WIDE),
        owned_up.T.astype(WIDE),
        owned_down.astype(WIDE),
        narrow[0],
        narrow[1],
        narrow[2],
        vectors[8 * width :],
        narrow[3],
        narrow[4],
        narrow[5],
        narrow[6],
        narrow[7],
    )


def solution(mesh):
    tokens = P("dp", "mp", None)
    by_rows, by_columns, whole = P("dp", "mp"), P("mp", "dp"), P()
    in_specs = (
        (tokens, P("dp", None), tokens)
        + (by_rows,) * 3
        + (by_columns, by_rows, by_columns)
        + (whole,) * 9
    )
    out_specs = (
        (tokens, tokens) + (by_rows,) * 3 + (by_columns, by_rows, by_columns) + (whole,) * 9
    )
    return jax.shard_map(body, mesh=mesh, in_specs=in_specs, out_specs=out_specs, check_vma=False)
```

profile of v0, /device:TPU:0, one launch (start us, length us, event | category | flops | bytes accessed | tf_op | source)
XLA Modules:
  0.0 1098.2 jit_solution(11047037456383570990)
XLA Ops:
  11.7 20.5 %all_to_all.144 = bf16[8,256,256]{2,1,0:T(8,128)(2,1)S(1)} all-to-all(bf16[8,256,256]{2,1,0:T(8,128)(2,1)S(1)} %bitcast.238), channel_id=1, replica_groups=mesh['dp'=8,'mp'=4] {'dp'}, dimensions={0} | all-to-all | bytes 2097152 | tf_op jit(solution)/shard_map/all_to_all | solution.py:986
  47.7 17.2 %collective-permute-done.3 = s32[4,1024]{1,0:T(4,128)S(1)} collective-permute-done((s32[4,1024]{1,0:T(4,128)S(1)}, s32[4,1024]{1,0:T(4,128)S(1)}, u32[]{:S(2)}, u32[]{:S(2)}) %collective-permute-start.3) | collective-permute-done | bytes 16416 | tf_op jit(solution)/shard_map/ppermute | solution.py:963
  74.1 100.6 %opening_gather.1 = (bf16[2048,2048]{1,0:T(8,128)(2,1)}, bf16[2048,2048]{1,0:T(8,128)(2,1)}, bf16[4,256,2048]{2,1,0:T(8,128)(2,1)}) custom-call(bf16[256,2048]{1,0:T(8,128)(2,1)} %get-tuple-element.75.refs_0_, bf16[256,2048]{1,0:T(8,128)(2,1)} %get-tuple-element.76.refs_1_, bf16[256,2048]{1,0:T(8,128)(2,1)} %bitcast.233), custom_call_target="tpu_custom_call" | custom-call | bytes 134217728 | tf_op jit(solution)/shard_map/opening_gather/pallas_call | solution.py:857
  179.8 8.6 all_to_all.145
  191.6 10.8 add_convert_fusion.3.refs_0_
  204.8 10.2 add_convert_fusion.2.refs_1_
  215.0 11.6 %attend_forward.2 = (bf16[2048,256]{1,0:T(8,128)(2,1)}, f32[4,2,512]{2,1,0:T(2,128)}) custom-call(bf16[2048,768]{1,0:T(8,128)(2,1)} %add_convert_fusion.3.refs_0_, bf16[2048,768]{1,0:T(8,128)(2,1)} %add_convert_fusion.2.refs_1_, s32[4,1024,1]{2,1,0:T(8,128)} %copy.121.refs_2_.refs_6_, s32[4,2,512]{2,1,0:T(2,128)} %bitcast.265), custom_call_target="tpu_custom_call" | custom-call | flops 2147483648 | bytes 8388608 | tf_op jit(solution)/shard_map/attend_forward/pallas_call | solution.py:132
  226.6 11.5 %attend_forward.3 = (bf16[2048,256]{1,0:T(8,128)(2,1)}, f32[4,2,512]{2,1,0:T(2,128)}) custom-call(bf16[2048,768]{1,0:T(8,128)(2,1)} %add_convert_fusion.3.refs_0_, bf16[2048,768]{1,0:T(8,128)(2,1)} %add_convert_fusion.2.refs_1_, s32[4,1024,1]{2,1,0:T(8,128)} %copy.121.refs_2_.refs_6_, s32[4,2,512]{2,1,0:T(2,128)} %bitcast.266), custom_call_target="tpu_custom_call" | custom-call | flops 2147483648 | bytes 8388608 | tf_op jit(solution)/shard_map/attend_forward/pallas_call | solution.py:132
  238.1 84.3 %product_scatter.4 = f32[2,256,2048]{2,1,0:T(8,128)} custom-call(bf16[2048,256]{1,0:T(8,128)(2,1)} %get-tuple-element.86.refs_0_, bf16[2048,256]{1,0:T(8,128)(2,1)} %get-tuple-element.87.refs_1_, bf16[256,2048]{1,0:T(8,128)(2,1)} %bitcast.252), custom_call_target="tpu_custom_call" | custom-call | flops 4294967296 | bytes 134217728 | tf_op jit(solution)/shard_map/product_scatter/pallas_call | solution.py:441
  329.0 9.2 all-gather.5.cloned.1.call-done.refs_2_
  343.2 83.1 %gather_product.3 = (bf16[2048,2048]{1,0:T(8,128)(2,1)}, bf16[2048,2048]{1,0:T(8,128)(2,1)}, f32[2048,1024]{1,0:T(8,128)}, f32[2048,1024]{1,0:T(8,128)}, bf16[20...) custom-call(bf16[256,2048]{1,0:T(8,128)(2,1)} %get-tuple-element.89.refs_0_, ...), custom_call_target="tpu_custom_call" | custom-call | flops 17179869184 | bytes 134217728 | tf_op jit(solution)/shard_map/gather_product/pallas_call | solution.py:673
  430.6 91.1 %product_scatter.5 = f32[2,256,2048]{2,1,0:T(8,128)} custom-call(bf16[2048,1024]{1,0:T(8,128)(2,1)} %get-tuple-element.95.refs_0_, bf16[2048,1024]{1,0:T(8,128)(2,1)} %get-tuple-element.96.refs_1_, bf16[1024,2048]{1,0:T(8,128)(2,1)} %all-gather.5.cloned.1.call-done.refs_2_), custom_call_target="tpu_custom_call" | custom-call | flops 17179869184 | bytes 134217728 | tf_op jit(solution)/shard_map/product_scatter/pallas_call | solution.py:441
  521.7 4.0 fusion.53
  532.4 9.4 collective-permute-start.7
  547.2 81.8 %gather_product.4 = (bf16[2048,2048]{1,0:T(8,128)(2,1)}, bf16[2048,2048]{1,0:T(8,128)(2,1)}, bf16[2048,1024]{1,0:T(8,128)(2,1)}, bf16[2048,1024]{1,0:T(8,128)(2,1)}) custom-call(bf16[256,2048]{1,0:T(8,128)(2,1)} %get-tuple-element.291.refs_0_, bf16[256,2048]{1,0:T(8,128)(2,1)} %get-tuple-element.218.refs_1_, ...), custom_call_target="tpu_custom_call" | custom-call | flops 17179869184 | bytes 134217728 | tf_op jit(solution)/shard_map/gather_product/pallas_call | solution.py:673
  633.0 12.0 %fusion.64 = f32[1024,2048]{1,0:T(8,128)S(1)} fusion(bf16[2048,1024]{1,0:T(8,128)(2,1)S(1)} %copy-done.29, bf16[2048,2048]{1,0:T(8,128)(2,1)} %get-tuple-element.112), kind=kOutput, calls=%fused_computation.190 | convolution fusion | flops 8589934592 | bytes 20971520 | tf_op jit(solution)/shard_map/dot_general | solution.py:20
  645.1 10.5 add_convert_fusion
  660.6 90.9 %product_scatter.6 = (f32[2,256,2048]{2,1,0:T(8,128)}, bf16[1024,2048]{1,0:T(8,128)(2,1)}) custom-call(bf16[2048,1024]{1,0:T(8,128)(2,1)} %get-tuple-element.107.refs_0_, bf16[2048,1024]{1,0:T(8,128)(2,1)} %get-tuple-element.108.refs_1_, bf16[1024,2048]{1,0:T(8,128)(2,1)} %all-gather.3.cloned.1.call-done.refs_2_, ...), custom_call_target="tpu_custom_call" | custom-call | flops 34359738368 | bytes 134217728 | tf_op jit(solution)/shard_map/product_scatter/pallas_call | solution.py:441
  751.5 4.9 multiply_reduce_fusion
  756.9 6.0 fusion.51
  765.3 74.9 %gather_product.5 = (bf16[2048,2048]{1,0:T(8,128)(2,1)}, bf16[2048,2048]{1,0:T(8,128)(2,1)}, bf16[2048,256]{1,0:T(8,128)(2,1)}, bf16[2048,256]{1,0:T(8,128)(2,1)}) custom-call(bf16[256,2048]{1,0:T(8,128)(2,1)} %get-tuple-element.114.refs_0_, bf16[256,2048]{1,0:T(8,128)(2,1)} %get-tuple-element.115.refs_1_, bf16[256,2048]{1,0:T(8,128)(2,1)} %bitcast.253), custom_call_target="tpu_custom_call" | custom-call | flops 4294967296 | bytes 134217728 | tf_op jit(solution)/shard_map/gather_product/pallas_call | solution.py:673
  840.2 32.2 %attend_backward.1 = (bf16[2048,768]{1,0:T(8,128)(2,1)}, bf16[2048,768]{1,0:T(8,128)(2,1)}, f32[4,1,768]{2,1,0:T(1,128)}) custom-call(bf16[2048,768]{1,0:T(8,128)(2,1)} %add_convert_fusion.3.refs_0_, bf16[2048,768]{1,0:T(8,128)(2,1)} %add_convert_fusion.2.refs_1_, bf16[2048,256]{1,0:T(8,128)(2,1)} %get-tuple-element.116.refs_2_, ...), custom_call_target="tpu_custom_call" | custom-call | flops 10737418240 | bytes 16777216 | tf_op jit(solution)/shard_map/attend_backward/pallas_call | solution.py:158
  874.2 5.9 fusion.66
  880.1 11.3 %fusion.65 = f32[768,2048]{1,0:T(8,128)} fusion(bf16[2048,768]{1,0:T(8,128)(2,1)S(1)} %copy-done.28, bf16[2048,2048]{1,0:T(8,128)(2,1)} %get-tuple-element.78), kind=kOutput, calls=%fused_computation.191 | convolution fusion | flops 6442450944 | bytes 17825792 | tf_op jit(solution)/shard_map/dot_general | solution.py:20
  894.8 5.6 all_to_all.146
  903.0 12.2 %add_convert_fusion.1 = bf16[768,2048]{1,0:T(8,128)(2,1)S(1)} fusion(f32[768,2048]{1,0:T(8,128)} %fusion.65, bf16[2048,768]{1,0:T(8,128)(2,1)} %get-tuple-element.126.refs_1_, bf16[2048,2048]{1,0:T(8,128)(2,1)} %get-tuple-element.83), kind=kOutput, calls=%fused_computation.3 | convolution fusion | flops 6445596672 | bytes 20971520 | tf_op jit(solution)/shard_map/dot_general | solution.py:20
  918.5 6.3 all_to_all.147
  935.5 89.7 %product_scatter.7 = f32[2,256,2048]{2,1,0:T(8,128)} custom-call(bf16[2048,768]{1,0:T(8,128)(2,1)} %get-tuple-element.125.refs_0_, bf16[2048,768]{1,0:T(8,128)(2,1)} %get-tuple-element.126.refs_1_, bf16[768,2048]{1,0:T(8,128)(2,1)} %bitcast.244), custom_call_target="tpu_custom_call" | custom-call | flops 12884901888 | bytes 134217728 | tf_op jit(solution)/shard_map/product_scatter/pallas_call | solution.py:441
  1025.2 4.4 all-to-all-start.8
  1035.2 9.4 collective-permute-start.11
  1066.4 4.2 all-to-all-start.4
  1075.9 5.2 collective-permute-done.12
  (243 shorter events, 142.9 us)
Async XLA Ops:
  35.2 139.4 %all-to-all-start.1 = ((bf16[8,512,256]{2,1,0:T(8,128)(2,1)}), bf16[8,512,256]{2,1,0:T(8,128)(2,1)S(1)}, u32[]{:S(2)}, u32[]{:S(2)}) async-start(bf16[8,512,256]{2,1,0:T(8,128)(2,1)} %pad_maximum_fusion), calls=%async_computation.1 | async-start | bytes 4194304 | tf_op jit(solution)/shard_map/all_to_all | solution.py:1008
  39.0 290.1 %all-gather.3.cloned.1.call-start = ((), (), s32[]{:S(2)}) async-start(), calls=%async_computation.13 | async-start | bytes 5242880 | tf_op jit(solution)/shard_map/all_gather | solution.py:1042
  39.0 7.0 collective-permute-start.2
  42.6 26.6 %collective-permute-start = (bf16[256,2048]{1,0:T(8,128)(2,1)}, bf16[256,2048]{1,0:T(8,128)(2,1)S(1)}, u32[]{:S(2)}, u32[]{:S(2)}) collective-permute-start(bf16[256,2048]{1,0:T(8,128)(2,1)} %get-tuple-element.260), channel_id=1, source_target_pairs={{0,0},{1,1},{2,4},{3,5},{4,2},{5,3},{6,6},{7,7},{8,8},{9,9},{10,12... | collective-permute-start | bytes 3145736 | tf_op jit(solution)/shard_map/ppermute | solution.py:942
  44.4 26.4 %collective-permute-start.1 = (bf16[256,2048]{1,0:T(8,128)(2,1)}, bf16[256,2048]{1,0:T(8,128)(2,1)}, u32[]{:S(2)}, u32[]{:S(2)}) collective-permute-start(bf16[256,2048]{1,0:T(8,128)(2,1)} %get-tuple-element.259), channel_id=1, source_target_pairs={{0,1},{1,0},{2,5},{3,4},{4,3},{5,2},{6,7},{7,6},{8,9},{9,8},{10,13... | collective-permute-start | bytes 3145736 | tf_op jit(solution)/shard_map/ppermute | solution.py:942
  46.0 18.9 %collective-permute-start.3 = (s32[4,1024]{1,0:T(4,128)S(1)}, s32[4,1024]{1,0:T(4,128)S(1)}, u32[]{:S(2)}, u32[]{:S(2)}) collective-permute-start(s32[4,1024]{1,0:T(4,128)S(1)} %pad_add_fusion.2), channel_id=1, source_target_pairs={{0,8},{4,12},{8,0},{12,4},{16,24},{20,28},{24,16},{28,20},{1,9},{5... | collective-permute-start | bytes 49160 | tf_op jit(solution)/shard_map/ppermute | solution.py:963
  65.0 4.0 collective-permute-start.4
  176.4 161.8 %all-gather.5.cloned.1.call-start = ((), (), s32[]{:S(2)}) async-start(), calls=%async_computation.14 | async-start | bytes 5242880 | tf_op jit(solution)/shard_map/all_gather | solution.py:1043
  191.1 574.2 %reduce-scatter.5.cloned.1.call-start = ((), (), s32[]{:S(2)}) async-start(), calls=%async_computation.15 | async-start | bytes 5242880 | tf_op jit(solution)/shard_map/reduce_scatter | solution.py:1080
  238.1 84.4 %copy-start.5 = (bf16[256,2048]{1,0:T(8,128)(2,1)S(1)}, bf16[256,2048]{1,0:T(8,128)(2,1)}, u32[]{:S(2)}) copy-start(bf16[256,2048]{1,0:T(8,128)(2,1)} %get-tuple-element.76.refs_1_) | copy-start | bytes 3145732
  238.1 84.4 %copy-start.23 = (f32[2048]{0:T(1024)S(1)}, f32[2048]{0:T(1024)}, u32[]{:S(2)}) copy-start(f32[2048]{0:T(1024)} %param.29) | copy-start | bytes 24580
  341.3 85.0 %collective-permute-start.5 = (bf16[256,2048]{1,0:T(8,128)(2,1)}, bf16[256,2048]{1,0:T(8,128)(2,1)S(1)}, u32[]{:S(2)}, u32[]{:S(2)}) collective-permute-start(bf16[256,2048]{1,0:T(8,128)(2,1)} %get-tuple-element.254), channel_id=1, source_target_pairs={{0,0},{1,1},{2,4},{3,5},{4,2},{5,3},{6,6},{7,7},{8,8},{9,9},{10,12... | collective-permute-start | bytes 3145736 | tf_op jit(solution)/shard_map/ppermute | solution.py:942
  343.2 83.2 %collective-permute-start.6 = (bf16[256,2048]{1,0:T(8,128)(2,1)}, bf16[256,2048]{1,0:T(8,128)(2,1)}, u32[]{:S(2)}, u32[]{:S(2)}) collective-permute-start(bf16[256,2048]{1,0:T(8,128)(2,1)} %get-tuple-element.253), channel_id=1, source_target_pairs={{0,1},{1,0},{2,5},{3,4},{4,3},{5,2},{6,7},{7,6},{8,9},{9,8},{10,13... | collective-permute-start | bytes 3145736 | tf_op jit(solution)/shard_map/ppermute | solution.py:942
  430.6 91.1 %copy-start.26 = (f32[2048]{0:T(1024)S(1)}, f32[2048]{0:T(1024)}, u32[]{:S(2)}) copy-start(f32[2048]{0:T(1024)} %param.31) | copy-start | bytes 24580
  532.4 96.6 %collective-permute-start.7 = (bf16[256,2048]{1,0:T(8,128)(2,1)}, bf16[256,2048]{1,0:T(8,128)(2,1)}, u32[]{:S(2)}, u32[]{:S(2)}) collective-permute-start(bf16[256,2048]{1,0:T(8,128)(2,1)} %get-tuple-element.250), channel_id=1, source_target_pairs={{0,0},{1,1},{4,2},{5,3},{2,4},{3,5},{6,6},{7,7},{8,8},{9,9},{12,10... | collective-permute-start | bytes 3145736 | tf_op jit(solution)/shard_map/ppermute | solution.py:956
  541.8 87.2 %collective-permute-start.8 = (bf16[256,2048]{1,0:T(8,128)(2,1)}, bf16[256,2048]{1,0:T(8,128)(2,1)}, u32[]{:S(2)}, u32[]{:S(2)}) collective-permute-start(bf16[256,2048]{1,0:T(8,128)(2,1)} %get-tuple-element.249), channel_id=1, source_target_pairs={{1,0},{0,1},{5,2},{4,3},{3,4},{2,5},{7,6},{6,7},{9,8},{8,9},{13,10... | collective-permute-start | bytes 3145736 | tf_op jit(solution)/shard_map/ppermute | solution.py:956
  655.6 259.6 %reduce-scatter.7.cloned.1.call-start = ((), (), s32[]{:S(2)}) async-start(), calls=%async_computation.16 | async-start | bytes 5242880 | tf_op jit(solution)/shard_map/reduce_scatter | solution.py:1080
  756.5 297.9 %reduce-scatter.11.cloned.1.call-start = ((), (), s32[]{:S(2)}) async-start(), calls=%async_computation.18 | async-start | bytes 1310720 | tf_op jit(solution)/shard_map/reduce_scatter | solution.py:1077
  840.2 33.2 %copy-start.9 = (bf16[256,2048]{1,0:T(8,128)(2,1)S(1)}, bf16[256,2048]{1,0:T(8,128)(2,1)}, u32[]{:S(2)}) copy-start(bf16[256,2048]{1,0:T(8,128)(2,1)} %get-tuple-element.114.refs_0_) | copy-start | bytes 3145732
  840.2 33.4 %copy-start.7 = (bf16[256,2048]{1,0:T(8,128)(2,1)S(1)}, bf16[256,2048]{1,0:T(8,128)(2,1)}, u32[]{:S(2)}) copy-start(bf16[256,2048]{1,0:T(8,128)(2,1)} %get-tuple-element.115.refs_1_) | copy-start | bytes 3145732
  873.9 28.1 %collective-permute-start.9 = (f32[192,128]{1,0:T(8,128)S(1)}, f32[192,128]{1,0:T(8,128)S(1)}, u32[]{:S(2)}, u32[]{:S(2)}) collective-permute-start(f32[192,128]{1,0:T(8,128)S(1)} %bitcast.263), channel_id=1, source_target_pairs={{0,1},{1,0},{2,3},{3,2},{4,5},{5,4},{6,7},{7,6},{8,9},{9,8},{10,11... | collective-permute-start | bytes 294920 | tf_op jit(solution)/shard_map/ppermute | solution.py:889
  901.9 158.3 %reduce-scatter.9.cloned.1.call-start = ((), (), s32[]{:S(2)}) async-start(), calls=%async_computation.17 | async-start | bytes 3932160 | tf_op jit(solution)/shard_map/reduce_scatter | solution.py:1161
  902.0 26.3 %collective-permute-start.10 = (f32[192,128]{1,0:T(8,128)S(1)}, f32[192,128]{1,0:T(8,128)S(1)}, u32[]{:S(2)}, u32[]{:S(2)}) collective-permute-start(f32[192,128]{1,0:T(8,128)S(1)} %bitcast_add_fusion.8), channel_id=1, source_target_pairs={{0,2},{1,3},{2,0},{3,1},{4,6},{5,7},{6,4},{7,5},{8,10},{9,11},{10,... | collective-permute-start | bytes 294920 | tf_op jit(solution)/shard_map/ppermute | solution.py:889
  930.5 94.7 %all-to-all-start.7 = ((bf16[256,8,256]{2,0,1:T(8,128)(2,1)}), bf16[256,8,256]{2,0,1:T(8,128)(2,1)S(1)}, u32[]{:S(2)}, u32[]{:S(2)}) async-start(bf16[256,8,256]{2,0,1:T(8,128)(2,1)} %bitcast.221), calls=%async_computation.11 | async-start | bytes 2097152 | tf_op jit(solution)/shard_map/all_to_all | solution.py:1083
  1025.2 30.9 %all-to-all-start.8 = ((bf16[256,8,256]{2,0,1:T(8,128)(2,1)}), bf16[256,8,256]{2,0,1:T(8,128)(2,1)}, u32[]{:S(2)}, u32[]{:S(2)}) async-start(bf16[256,8,256]{2,0,1:T(8,128)(2,1)} %bitcast.237), calls=%async_computation.12 | async-start | bytes 2097152 | tf_op jit(solution)/shard_map/all_to_all | solution.py:1083
  1035.2 40.8 %collective-permute-start.11 = (bf16[256,2048]{1,0:T(8,128)(2,1)}, bf16[256,2048]{1,0:T(8,128)(2,1)}, u32[]{:S(2)}, u32[]{:S(2)}) collective-permute-start(bf16[256,2048]{1,0:T(8,128)(2,1)} %get-tuple-element.246), channel_id=1, source_target_pairs={{0,0},{1,1},{4,2},{5,3},{2,4},{3,5},{6,6},{7,7},{8,8},{9,9},{12,10... | collective-permute-start | bytes 3145736 | tf_op jit(solution)/shard_map/ppermute | solution.py:956
  1044.6 36.5 %collective-permute-start.12 = (bf16[256,2048]{1,0:T(8,128)(2,1)}, bf16[256,2048]{1,0:T(8,128)(2,1)}, u32[]{:S(2)}, u32[]{:S(2)}) collective-permute-start(bf16[256,2048]{1,0:T(8,128)(2,1)} %get-tuple-element.245), channel_id=1, source_target_pairs={{1,0},{0,1},{5,2},{4,3},{3,4},{2,5},{7,6},{6,7},{9,8},{8,9},{13,10... | collective-permute-start | bytes 3145736 | tf_op jit(solution)/shard_map/ppermute | solution.py:956
  1046.1 1.3 collective-permute-start.13
  1047.5 5.1 collective-permute-start.14
  1052.5 7.0 collective-permute-start.15
  1056.1 10.3 all-to-all-start.6
  1066.4 20.1 %all-to-all-start.4 = ((bf16[192,8,256]{2,0,1:T(8,128)(2,1)}), bf16[192,8,256]{2,0,1:T(8,128)(2,1)}, u32[]{:S(2)}, u32[]{:S(2)}) async-start(bf16[192,8,256]{2,0,1:T(8,128)(2,1)} %copy.127), calls=%async_computation.7 | async-start | bytes 1572864 | tf_op jit(solution)/shard_map/all_to_all | solution.py:1083
  (29 other events, 200.6 us)
Sparse Core Ops, SparseCore 0:
  176.5 80.8 all-gather.2
  258.9 79.2 all-gather.4
  655.8 73.9 reduce-scatter.4
  756.6 74.4 reduce-scatter.6
  902.0 26.5 reduce-scatter.10
  930.8 58.9 reduce-scatter.8
where the time goes:
time: 1110 us; the launch traced here: 1100 us
  Pallas kernels  752 us (68%)
  matrix products  75.3 us (7%)
  other arithmetic  63.6 us (6%)
  starting transfers between devices  57.9 us (5%)
  local copies, waits for them, and re-layouts  49.1 us (4%)
  waiting for transfers between devices  43.9 us (4%)
  blocking collectives  40.9 us (4%)
  between operations  15.7 us (1%)
    pallas_call x4, Pallas kernels, product_scatter(): pl.pallas_call(functools.partial(scatter_kernel, bits, parts, side), out_...  356 us
    pallas_call x3, Pallas kernels, gather_product(): pl.pallas_call(functools.partial(gather_kernel, bits, parts, mode), out_s...  240 us
    pallas_call x1, Pallas kernels, opening_gather(): pl.pallas_call(functools.partial(opening_kernel, bits, parts, depth), out...  101 us
    dot_general x8, matrix products, contract(): lax.dot_general(left, right, (((left_dim,), (right_dim,)), ((), ())), pre...  75.3 us
    pallas_call x1, Pallas kernels, attend_backward(): pl.pallas_call(functools.partial(backward_kernel, heads, parts), grid=(se...  32.2 us
    pallas_call x2, Pallas kernels, attend_forward(): pl.pallas_call(functools.partial(forward_kernel, heads, parts, which), gr...  23.1 us
    ppermute x4, starting transfers between devices, leave_sent(): lax.ppermute(picks[turn], ('dp', 'mp'), route(turn, True))  22.8 us
  transfers between devices with their start and end apart: 27, of which 8 were waited for; matrix products, arithmetic and copies ran while one was open for 11% of the time, Pallas kernels for 60%

commit v1 on v0

--- a/solution.py
+++ b/solution.py
@@ -391,7 +391,7 @@
         if (part, pattern) not in urgent
     ]
     queue = urgent + others
-    ahead = 2 * parts
+    ahead = parts
     for entry in queue[:ahead]:
         far_tile(*entry)
     for number, (part, pattern) in enumerate(queue):
@@ -1052,14 +1052,12 @@
         for b in every
     ]
     first_low = [first[b][0].astype(LOW) for b in every]
-    first_low, full_up, full_down, cotangent = together(
-        (first_low, full_up, full_down, cotangent)
-    )
+    first_low, full_up, cotangent = together((first_low, full_up, cotangent))
     tangents = enter(cotangent)
     gathered_first, up_proj, hiddens = gather_product(
         first_low, full_up, own_up.reshape(1, -1), 4
     )
-    hiddens, tangents = together((hiddens, tangents))
+    hiddens, tangents, full_down = together((hiddens, tangents, full_down))
     tangents = [array.astype(WIDE) for array in tangents]
     ffn_sums = product_scatter(hiddens, full_down, 2)
     second = [

time: 1110 us -> 1100 us (level)
  transfers between devices with their start and end apart: 27 -> 27, of which waited for: 8 -> 7; matrix products, arithmetic and copies ran while one was open for 11% -> 12% of each run, Pallas kernels for 60% -> 61%
where the time goes in v1:
time: 1100 us; the launch traced here: 1090 us
  Pallas kernels  750 us (68%)
  matrix products  75.4 us (7%)
  other arithmetic  63.4 us (6%)
  starting transfers between devices  57.9 us (5%)
  local copies, waits for them, and re-layouts  48.6 us (4%)
  blocking collectives  40.4 us (4%)
  waiting for transfers between devices  35.4 us (3%)
  between operations  15.7 us (1%)
    pallas_call x4, Pallas kernels, product_scatter(): pl.pallas_call(functools.partial(scatter_kernel, bits, parts, side), out_...  353 us
    pallas_call x3, Pallas kernels, gather_product(): pl.pallas_call(functools.partial(gather_kernel, bits, parts, mode), out_s...  241 us
    pallas_call x1, Pallas kernels, opening_gather(): pl.pallas_call(functools.partial(opening_kernel, bits, parts, depth), out...  101 us
    dot_general x8, matrix products, contract(): lax.dot_general(left, right, (((left_dim,), (right_dim,)), ((), ())), pre...  75.4 us
    pallas_call x1, Pallas kernels, attend_backward(): pl.pallas_call(functools.partial(backward_kernel, heads, parts), grid=(se...  32.2 us
    pallas_call x2, Pallas kernels, attend_forward(): pl.pallas_call(functools.partial(forward_kernel, heads, parts, which), gr...  23.1 us
  transfers between devices with their start and end apart: 27, of which 7 were waited for; matrix products, arithmetic and copies ran while one was open for 12% of the time, Pallas kernels for 61%

profile of v1, /device:TPU:0, one launch (start us, length us, event | category | flops | bytes accessed | tf_op | source)
XLA Modules:
  0.0 1087.3 jit_solution(6994193913512589438)
XLA Ops:
  11.7 20.5 %all_to_all.144 = bf16[8,256,256]{2,1,0:T(8,128)(2,1)S(1)} all-to-all(bf16[8,256,256]{2,1,0:T(8,128)(2,1)S(1)} %bitcast.238), channel_id=1, replica_groups=mesh['dp'=8,'mp'=4] {'dp'}, dimensions={0} | all-to-all | bytes 2097152 | tf_op jit(solution)/shard_map/all_to_all | solution.py:986
  47.7 17.2 %collective-permute-done.3 = s32[4,1024]{1,0:T(4,128)S(1)} collective-permute-done((s32[4,1024]{1,0:T(4,128)S(1)}, s32[4,1024]{1,0:T(4,128)S(1)}, u32[]{:S(2)}, u32[]{:S(2)}) %collective-permute-start.3) | collective-permute-done | bytes 16416 | tf_op jit(solution)/shard_map/ppermute | solution.py:963
  74.1 100.6 %opening_gather.1 = (bf16[2048,2048]{1,0:T(8,128)(2,1)}, bf16[2048,2048]{1,0:T(8,128)(2,1)}, bf16[4,256,2048]{2,1,0:T(8,128)(2,1)}) custom-call(bf16[256,2048]{1,0:T(8,128)(2,1)} %get-tuple-element.75.refs_0_, bf16[256,2048]{1,0:T(8,128)(2,1)} %get-tuple-element.76.refs_1_, bf16[256,2048]{1,0:T(8,128)(2,1)} %bitcast.233), custom_call_target="tpu_custom_call" | custom-call | bytes 134217728 | tf_op jit(solution)/shard_map/opening_gather/pallas_call | solution.py:857
  179.8 8.6 all_to_all.145
  191.6 10.8 add_convert_fusion.3.refs_0_
  202.4 10.3 add_convert_fusion.2.refs_1_
  215.1 11.6 %attend_forward.2 = (bf16[2048,256]{1,0:T(8,128)(2,1)}, f32[4,2,512]{2,1,0:T(2,128)}) custom-call(bf16[2048,768]{1,0:T(8,128)(2,1)} %add_convert_fusion.3.refs_0_, bf16[2048,768]{1,0:T(8,128)(2,1)} %add_convert_fusion.2.refs_1_, s32[4,1024,1]{2,1,0:T(8,128)} %copy.121.refs_2_.refs_6_, s32[4,2,512]{2,1,0:T(2,128)} %bitcast.265), custom_call_target="tpu_custom_call" | custom-call | flops 2147483648 | bytes 8388608 | tf_op jit(solution)/shard_map/attend_forward/pallas_call | solution.py:132
  226.6 11.6 %attend_forward.3 = (bf16[2048,256]{1,0:T(8,128)(2,1)}, f32[4,2,512]{2,1,0:T(2,128)}) custom-call(bf16[2048,768]{1,0:T(8,128)(2,1)} %add_convert_fusion.3.refs_0_, bf16[2048,768]{1,0:T(8,128)(2,1)} %add_convert_fusion.2.refs_1_, s32[4,1024,1]{2,1,0:T(8,128)} %copy.121.refs_2_.refs_6_, s32[4,2,512]{2,1,0:T(2,128)} %bitcast.266), custom_call_target="tpu_custom_call" | custom-call | flops 2147483648 | bytes 8388608 | tf_op jit(solution)/shard_map/attend_forward/pallas_call | solution.py:132
  238.2 85.1 %product_scatter.4 = f32[2,256,2048]{2,1,0:T(8,128)} custom-call(bf16[2048,256]{1,0:T(8,128)(2,1)} %get-tuple-element.86.refs_0_, bf16[2048,256]{1,0:T(8,128)(2,1)} %get-tuple-element.87.refs_1_, bf16[256,2048]{1,0:T(8,128)(2,1)} %bitcast.252), custom_call_target="tpu_custom_call" | custom-call | flops 4294967296 | bytes 134217728 | tf_op jit(solution)/shard_map/product_scatter/pallas_call | solution.py:441
  334.8 83.4 %gather_product.3 = (bf16[2048,2048]{1,0:T(8,128)(2,1)}, bf16[2048,2048]{1,0:T(8,128)(2,1)}, f32[2048,1024]{1,0:T(8,128)}, f32[2048,1024]{1,0:T(8,128)}, bf16[20...) custom-call(bf16[256,2048]{1,0:T(8,128)(2,1)} %get-tuple-element.89.refs_0_, ...), custom_call_target="tpu_custom_call" | custom-call | flops 17179869184 | bytes 134217728 | tf_op jit(solution)/shard_map/gather_product/pallas_call | solution.py:673
  422.4 89.6 %product_scatter.5 = f32[2,256,2048]{2,1,0:T(8,128)} custom-call(bf16[2048,1024]{1,0:T(8,128)(2,1)} %get-tuple-element.95.refs_0_, bf16[2048,1024]{1,0:T(8,128)(2,1)} %get-tuple-element.96.refs_1_, bf16[1024,2048]{1,0:T(8,128)(2,1)} %all-gather.5.cloned.1.call-done.refs_2_), custom_call_target="tpu_custom_call" | custom-call | flops 17179869184 | bytes 134217728 | tf_op jit(solution)/shard_map/product_scatter/pallas_call | solution.py:441
  512.0 4.0 fusion.53
  522.7 9.4 collective-permute-start.7
  536.6 81.4 %gather_product.4 = (bf16[2048,2048]{1,0:T(8,128)(2,1)}, bf16[2048,2048]{1,0:T(8,128)(2,1)}, bf16[2048,1024]{1,0:T(8,128)(2,1)}, bf16[2048,1024]{1,0:T(8,128)(2,1)}) custom-call(bf16[256,2048]{1,0:T(8,128)(2,1)} %get-tuple-element.291.refs_0_, bf16[256,2048]{1,0:T(8,128)(2,1)} %get-tuple-element.218.refs_1_, ...), custom_call_target="tpu_custom_call" | custom-call | flops 17179869184 | bytes 134217728 | tf_op jit(solution)/shard_map/gather_product/pallas_call | solution.py:673
  622.0 12.0 %fusion.64 = f32[1024,2048]{1,0:T(8,128)S(1)} fusion(bf16[2048,1024]{1,0:T(8,128)(2,1)S(1)} %copy-done.29, bf16[2048,2048]{1,0:T(8,128)(2,1)} %get-tuple-element.112), kind=kOutput, calls=%fused_computation.190 | convolution fusion | flops 8589934592 | bytes 20971520 | tf_op jit(solution)/shard_map/dot_general | solution.py:20
  634.1 10.5 add_convert_fusion
  649.2 90.2 %product_scatter.6 = (f32[2,256,2048]{2,1,0:T(8,128)}, bf16[1024,2048]{1,0:T(8,128)(2,1)}) custom-call(bf16[2048,1024]{1,0:T(8,128)(2,1)} %get-tuple-element.107.refs_0_, bf16[2048,1024]{1,0:T(8,128)(2,1)} %get-tuple-element.108.refs_1_, bf16[1024,2048]{1,0:T(8,128)(2,1)} %all-gather.3.cloned.1.call-done.refs_2_, ...), custom_call_target="tpu_custom_call" | custom-call | flops 34359738368 | bytes 134217728 | tf_op jit(solution)/shard_map/product_scatter/pallas_call | solution.py:441
  739.3 4.9 multiply_reduce_fusion
  744.8 5.8 fusion.51
  752.9 76.6 %gather_product.5 = (bf16[2048,2048]{1,0:T(8,128)(2,1)}, bf16[2048,2048]{1,0:T(8,128)(2,1)}, bf16[2048,256]{1,0:T(8,128)(2,1)}, bf16[2048,256]{1,0:T(8,128)(2,1)}) custom-call(bf16[256,2048]{1,0:T(8,128)(2,1)} %get-tuple-element.114.refs_0_, bf16[256,2048]{1,0:T(8,128)(2,1)} %get-tuple-element.115.refs_1_, bf16[256,2048]{1,0:T(8,128)(2,1)} %bitcast.253), custom_call_target="tpu_custom_call" | custom-call | flops 4294967296 | bytes 134217728 | tf_op jit(solution)/shard_map/gather_product/pallas_call | solution.py:673
  829.6 32.2 %attend_backward.1 = (bf16[2048,768]{1,0:T(8,128)(2,1)}, bf16[2048,768]{1,0:T(8,128)(2,1)}, f32[4,1,768]{2,1,0:T(1,128)}) custom-call(bf16[2048,768]{1,0:T(8,128)(2,1)} %add_convert_fusion.3.refs_0_, bf16[2048,768]{1,0:T(8,128)(2,1)} %add_convert_fusion.2.refs_1_, bf16[2048,256]{1,0:T(8,128)(2,1)} %get-tuple-element.116.refs_2_, ...), custom_call_target="tpu_custom_call" | custom-call | flops 10737418240 | bytes 16777216 | tf_op jit(solution)/shard_map/attend_backward/pallas_call | solution.py:158
  864.2 5.9 fusion.66
  870.1 11.3 %fusion.65 = f32[768,2048]{1,0:T(8,128)} fusion(bf16[2048,768]{1,0:T(8,128)(2,1)S(1)} %copy-done.28, bf16[2048,2048]{1,0:T(8,128)(2,1)} %get-tuple-element.78), kind=kOutput, calls=%fused_computation.191 | convolution fusion | flops 6442450944 | bytes 17825792 | tf_op jit(solution)/shard_map/dot_general | solution.py:20
  884.9 5.1 all_to_all.146
  893.0 12.3 %add_convert_fusion.1 = bf16[768,2048]{1,0:T(8,128)(2,1)S(1)} fusion(f32[768,2048]{1,0:T(8,128)} %fusion.65, bf16[2048,768]{1,0:T(8,128)(2,1)} %get-tuple-element.126.refs_1_, bf16[2048,2048]{1,0:T(8,128)(2,1)} %get-tuple-element.83), kind=kOutput, calls=%fused_computation.3 | convolution fusion | flops 6445596672 | bytes 20971520 | tf_op jit(solution)/shard_map/dot_general | solution.py:20
  908.6 6.3 all_to_all.147
  920.6 3.8 all-to-all-start.7
  925.6 88.4 %product_scatter.7 = f32[2,256,2048]{2,1,0:T(8,128)} custom-call(bf16[2048,768]{1,0:T(8,128)(2,1)} %get-tuple-element.125.refs_0_, bf16[2048,768]{1,0:T(8,128)(2,1)} %get-tuple-element.126.refs_1_, bf16[768,2048]{1,0:T(8,128)(2,1)} %bitcast.244), custom_call_target="tpu_custom_call" | custom-call | flops 12884901888 | bytes 134217728 | tf_op jit(solution)/shard_map/product_scatter/pallas_call | solution.py:441
  1014.0 4.4 all-to-all-start.8
  1023.9 9.4 collective-permute-start.11
  1054.8 4.2 all-to-all-start.4
  1064.4 5.8 collective-permute-done.12
  (243 shorter events, 138.6 us)
Async XLA Ops:
  35.2 139.4 %all-to-all-start.1 = ((bf16[8,512,256]{2,1,0:T(8,128)(2,1)}), bf16[8,512,256]{2,1,0:T(8,128)(2,1)S(1)}, u32[]{:S(2)}, u32[]{:S(2)}) async-start(bf16[8,512,256]{2,1,0:T(8,128)(2,1)} %pad_maximum_fusion), calls=%async_computation.1 | async-start | bytes 4194304 | tf_op jit(solution)/shard_map/all_to_all | solution.py:1008
  39.0 290.8 %all-gather.3.cloned.1.call-start = ((), (), s32[]{:S(2)}) async-start(), calls=%async_computation.13 | async-start | bytes 5242880 | tf_op jit(solution)/shard_map/all_gather | solution.py:1042
  39.0 7.0 collective-permute-start.2
  42.6 26.6 %collective-permute-start = (bf16[256,2048]{1,0:T(8,128)(2,1)}, bf16[256,2048]{1,0:T(8,128)(2,1)S(1)}, u32[]{:S(2)}, u32[]{:S(2)}) collective-permute-start(bf16[256,2048]{1,0:T(8,128)(2,1)} %get-tuple-element.260), channel_id=1, source_target_pairs={{0,0},{1,1},{2,4},{3,5},{4,2},{5,3},{6,6},{7,7},{8,8},{9,9},{10,12... | collective-permute-start | bytes 3145736 | tf_op jit(solution)/shard_map/ppermute | solution.py:942
  44.4 26.4 %collective-permute-start.1 = (bf16[256,2048]{1,0:T(8,128)(2,1)}, bf16[256,2048]{1,0:T(8,128)(2,1)}, u32[]{:S(2)}, u32[]{:S(2)}) collective-permute-start(bf16[256,2048]{1,0:T(8,128)(2,1)} %get-tuple-element.259), channel_id=1, source_target_pairs={{0,1},{1,0},{2,5},{3,4},{4,3},{5,2},{6,7},{7,6},{8,9},{9,8},{10,13... | collective-permute-start | bytes 3145736 | tf_op jit(solution)/shard_map/ppermute | solution.py:942
  46.0 18.9 %collective-permute-start.3 = (s32[4,1024]{1,0:T(4,128)S(1)}, s32[4,1024]{1,0:T(4,128)S(1)}, u32[]{:S(2)}, u32[]{:S(2)}) collective-permute-start(s32[4,1024]{1,0:T(4,128)S(1)} %pad_add_fusion.2), channel_id=1, source_target_pairs={{0,8},{4,12},{8,0},{12,4},{16,24},{20,28},{24,16},{28,20},{1,9},{5... | collective-permute-start | bytes 49160 | tf_op jit(solution)/shard_map/ppermute | solution.py:963
  65.0 4.0 collective-permute-start.4
  176.4 246.0 %all-gather.5.cloned.1.call-start = ((), (), s32[]{:S(2)}) async-start(), calls=%async_computation.14 | async-start | bytes 5242880 | tf_op jit(solution)/shard_map/all_gather | solution.py:1043
  191.1 561.9 %reduce-scatter.5.cloned.1.call-start = ((), (), s32[]{:S(2)}) async-start(), calls=%async_computation.15 | async-start | bytes 5242880 | tf_op jit(solution)/shard_map/reduce_scatter | solution.py:1078
  238.2 85.1 %copy-start.5 = (bf16[256,2048]{1,0:T(8,128)(2,1)S(1)}, bf16[256,2048]{1,0:T(8,128)(2,1)}, u32[]{:S(2)}) copy-start(bf16[256,2048]{1,0:T(8,128)(2,1)} %get-tuple-element.76.refs_1_) | copy-start | bytes 3145732
  238.2 85.1 %copy-start.23 = (f32[2048]{0:T(1024)S(1)}, f32[2048]{0:T(1024)}, u32[]{:S(2)}) copy-start(f32[2048]{0:T(1024)} %param.29) | copy-start | bytes 24580
  332.9 85.2 %collective-permute-start.5 = (bf16[256,2048]{1,0:T(8,128)(2,1)}, bf16[256,2048]{1,0:T(8,128)(2,1)S(1)}, u32[]{:S(2)}, u32[]{:S(2)}) collective-permute-start(bf16[256,2048]{1,0:T(8,128)(2,1)} %get-tuple-element.256), channel_id=1, source_target_pairs={{0,0},{1,1},{2,4},{3,5},{4,2},{5,3},{6,6},{7,7},{8,8},{9,9},{10,12... | collective-permute-start | bytes 3145736 | tf_op jit(solution)/shard_map/ppermute | solution.py:942
  334.8 83.4 %collective-permute-start.6 = (bf16[256,2048]{1,0:T(8,128)(2,1)}, bf16[256,2048]{1,0:T(8,128)(2,1)}, u32[]{:S(2)}, u32[]{:S(2)}) collective-permute-start(bf16[256,2048]{1,0:T(8,128)(2,1)} %get-tuple-element.255), channel_id=1, source_target_pairs={{0,1},{1,0},{2,5},{3,4},{4,3},{5,2},{6,7},{7,6},{8,9},{9,8},{10,13... | collective-permute-start | bytes 3145736 | tf_op jit(solution)/shard_map/ppermute | solution.py:942
  422.4 89.6 %copy-start.26 = (f32[2048]{0:T(1024)S(1)}, f32[2048]{0:T(1024)}, u32[]{:S(2)}) copy-start(f32[2048]{0:T(1024)} %param.31) | copy-start | bytes 24580
  522.7 95.4 %collective-permute-start.7 = (bf16[256,2048]{1,0:T(8,128)(2,1)}, bf16[256,2048]{1,0:T(8,128)(2,1)}, u32[]{:S(2)}, u32[]{:S(2)}) collective-permute-start(bf16[256,2048]{1,0:T(8,128)(2,1)} %get-tuple-element.250), channel_id=1, source_target_pairs={{0,0},{1,1},{4,2},{5,3},{2,4},{3,5},{6,6},{7,7},{8,8},{9,9},{12,10... | collective-permute-start | bytes 3145736 | tf_op jit(solution)/shard_map/ppermute | solution.py:956
  532.1 85.9 %collective-permute-start.8 = (bf16[256,2048]{1,0:T(8,128)(2,1)}, bf16[256,2048]{1,0:T(8,128)(2,1)}, u32[]{:S(2)}, u32[]{:S(2)}) collective-permute-start(bf16[256,2048]{1,0:T(8,128)(2,1)} %get-tuple-element.249), channel_id=1, source_target_pairs={{1,0},{0,1},{5,2},{4,3},{3,4},{2,5},{7,6},{6,7},{9,8},{8,9},{13,10... | collective-permute-start | bytes 3145736 | tf_op jit(solution)/shard_map/ppermute | solution.py:956
  644.7 260.6 %reduce-scatter.7.cloned.1.call-start = ((), (), s32[]{:S(2)}) async-start(), calls=%async_computation.16 | async-start | bytes 5242880 | tf_op jit(solution)/shard_map/reduce_scatter | solution.py:1078
  744.3 298.5 %reduce-scatter.11.cloned.1.call-start = ((), (), s32[]{:S(2)}) async-start(), calls=%async_computation.18 | async-start | bytes 1310720 | tf_op jit(solution)/shard_map/reduce_scatter | solution.py:1075
  829.5 33.2 %copy-start.9 = (bf16[256,2048]{1,0:T(8,128)(2,1)S(1)}, bf16[256,2048]{1,0:T(8,128)(2,1)}, u32[]{:S(2)}) copy-start(bf16[256,2048]{1,0:T(8,128)(2,1)} %get-tuple-element.114.refs_0_) | copy-start | bytes 3145732
  829.5 33.4 %copy-start.7 = (bf16[256,2048]{1,0:T(8,128)(2,1)S(1)}, bf16[256,2048]{1,0:T(8,128)(2,1)}, u32[]{:S(2)}) copy-start(bf16[256,2048]{1,0:T(8,128)(2,1)} %get-tuple-element.115.refs_1_) | copy-start | bytes 3145732
  863.2 28.3 %collective-permute-start.9 = (f32[192,128]{1,0:T(8,128)S(1)}, f32[192,128]{1,0:T(8,128)S(1)}, u32[]{:S(2)}, u32[]{:S(2)}) collective-permute-start(f32[192,128]{1,0:T(8,128)S(1)} %bitcast.263), channel_id=1, source_target_pairs={{0,1},{1,0},{2,3},{3,2},{4,5},{5,4},{6,7},{7,6},{8,9},{9,8},{10,11... | collective-permute-start | bytes 294920 | tf_op jit(solution)/shard_map/ppermute | solution.py:889
  891.4 157.3 %reduce-scatter.9.cloned.1.call-start = ((), (), s32[]{:S(2)}) async-start(), calls=%async_computation.17 | async-start | bytes 3932160 | tf_op jit(solution)/shard_map/reduce_scatter | solution.py:1159
  891.5 26.8 %collective-permute-start.10 = (f32[192,128]{1,0:T(8,128)S(1)}, f32[192,128]{1,0:T(8,128)S(1)}, u32[]{:S(2)}, u32[]{:S(2)}) collective-permute-start(f32[192,128]{1,0:T(8,128)S(1)} %bitcast_add_fusion.8), channel_id=1, source_target_pairs={{0,2},{1,3},{2,0},{3,1},{4,6},{5,7},{6,4},{7,5},{8,10},{9,11},{10,... | collective-permute-start | bytes 294920 | tf_op jit(solution)/shard_map/ppermute | solution.py:889
  920.6 93.4 %all-to-all-start.7 = ((bf16[256,8,256]{2,0,1:T(8,128)(2,1)}), bf16[256,8,256]{2,0,1:T(8,128)(2,1)S(1)}, u32[]{:S(2)}, u32[]{:S(2)}) async-start(bf16[256,8,256]{2,0,1:T(8,128)(2,1)} %bitcast.221), calls=%async_computation.11 | async-start | bytes 2097152 | tf_op jit(solution)/shard_map/all_to_all | solution.py:1081
  1014.0 30.6 %all-to-all-start.8 = ((bf16[256,8,256]{2,0,1:T(8,128)(2,1)}), bf16[256,8,256]{2,0,1:T(8,128)(2,1)}, u32[]{:S(2)}, u32[]{:S(2)}) async-start(bf16[256,8,256]{2,0,1:T(8,128)(2,1)} %bitcast.237), calls=%async_computation.12 | async-start | bytes 2097152 | tf_op jit(solution)/shard_map/all_to_all | solution.py:1081
  1023.9 40.5 %collective-permute-start.11 = (bf16[256,2048]{1,0:T(8,128)(2,1)}, bf16[256,2048]{1,0:T(8,128)(2,1)}, u32[]{:S(2)}, u32[]{:S(2)}) collective-permute-start(bf16[256,2048]{1,0:T(8,128)(2,1)} %get-tuple-element.246), channel_id=1, source_target_pairs={{0,0},{1,1},{4,2},{5,3},{2,4},{3,5},{6,6},{7,7},{8,8},{9,9},{12,10... | collective-permute-start | bytes 3145736 | tf_op jit(solution)/shard_map/ppermute | solution.py:956
  1033.4 36.8 %collective-permute-start.12 = (bf16[256,2048]{1,0:T(8,128)(2,1)}, bf16[256,2048]{1,0:T(8,128)(2,1)}, u32[]{:S(2)}, u32[]{:S(2)}) collective-permute-start(bf16[256,2048]{1,0:T(8,128)(2,1)} %get-tuple-element.245), channel_id=1, source_target_pairs={{1,0},{0,1},{5,2},{4,3},{3,4},{2,5},{7,6},{6,7},{9,8},{8,9},{13,10... | collective-permute-start | bytes 3145736 | tf_op jit(solution)/shard_map/ppermute | solution.py:956
  1034.6 1.3 collective-permute-start.13
  1035.9 5.1 collective-permute-start.14
  1041.0 7.0 collective-permute-start.15
  1044.6 10.3 all-to-all-start.6
  1054.8 20.8 %all-to-all-start.4 = ((bf16[192,8,256]{2,0,1:T(8,128)(2,1)}), bf16[192,8,256]{2,0,1:T(8,128)(2,1)}, u32[]{:S(2)}, u32[]{:S(2)}) async-start(bf16[192,8,256]{2,0,1:T(8,128)(2,1)} %copy.127), calls=%async_computation.7 | async-start | bytes 1572864 | tf_op jit(solution)/shard_map/all_to_all | solution.py:1081
  (29 other events, 196.7 us)
Sparse Core Ops, SparseCore 0:
  176.5 80.8 all-gather.2
  258.9 79.2 all-gather.4
  644.8 74.6 reduce-scatter.4
  744.4 75.3 reduce-scatter.6
  891.5 26.0 reduce-scatter.10
  919.8 58.8 reduce-scatter.8
